TPU v7x, 512 devices: a whole 4x8x8 slice. The times are simulated.
512 devices in a mesh: dp: 64 (over x, z, y_lo), tp: 8 (over y_hi, core).
Axes of the slice: x: 4, y: 8 (y_hi: 4, y_lo: 2; y = y_hi * 2 + y_lo), z: 8, core: 2. Of those that a mesh axis runs over, the one named last changes fastest.
Arguments:
- stash_values: bfloat16 [65536, 8192], P(('dp', 'tp')), may hold values from -127 to 127
- stash_scales: bfloat16 [65536, 64], P(('dp', 'tp')), may hold values from 0.001 to 0.13
- value_grad: bfloat16 [65536, 1024], P('dp', 'tp'), may hold values from -19 to 19
Outputs:
- clipped_grad: float32 [8192, 1024], P('dp', 'tp')
All inputs are finite; a program needn't handle non-finite values.
Results may differ from a plain program's by a relative error of at most 0.0019.
Values may be sent and summed in bfloat16 or wider, within the bound.
A program may use at most 64 MiB of HBM per device.

v0:
```python
import jax
import jax.numpy as jnp
from jax import lax
from jax.sharding import Mesh
from jax.sharding import PartitionSpec as P

DP = ("dp_0", "dp_1", "dp_2")
TP = ("tp_0", "tp_1")
DP_TP = ("dp_0", "dp_1", "dp_2", "tp_0", "tp_1")


def copy_for_each(shard, axis):
    copies = jnp.broadcast_to(shard, (lax.axis_size(axis), *shard.shape))
    return lax.all_to_all(copies, axis, split_axis=0, concat_axis=0, tiled=True)


def in_order(pieces, dim):
    pieces = jnp.moveaxis(pieces, 0, dim)
    shape = pieces.shape
    return pieces.reshape(*shape[:dim], shape[dim] * shape[dim + 1], *shape[dim + 2 :])


def collect(shard, axis, dim):
    pieces = copy_for_each(shard, axis)
    return in_order(pieces, dim)


def split_up(shard, dim, size):
    shape = shard.shape
    pieces = shard.reshape(*shape[:dim], size, shape[dim] // size, *shape[dim + 1 :])
    return jnp.moveaxis(pieces, dim, 0)


def sent_and_summed(shard, axis, dim):
    pieces = split_up(shard, dim, lax.axis_size(axis))
    arrived = lax.all_to_all(pieces, axis, split_axis=0, concat_axis=0, tiled=True)
    return arrived.astype(jnp.float32).sum(axis=0)


def over_axes(shard, axes):
    for axis in axes:
        shard = lax.psum(shard, axis)
    return shard


def block_dequantize(values, scales):
    rows = values.shape[0]
    blocks = scales.shape[1]
    scaled = (
        values.astype(jnp.float32).reshape(rows, blocks, values.shape[1] // blocks)
        * scales.astype(jnp.float32)[:, :, None]
    )
    return scaled.reshape(rows, values.shape[1]).astype(jnp.bfloat16)


def body(stash_values, stash_scales, value_grad):
    width = stash_values.shape[1]
    columns = value_grad.shape[1]
    dp_count = lax.axis_size(DP)
    tp_count = lax.axis_size(TP)
    own_tokens = stash_values.shape[0]
    sub_rows = width // (dp_count * tp_count)
    inputs = block_dequantize(stash_values, stash_scales)
    inputs = inputs.reshape(own_tokens, dp_count, tp_count, sub_rows)
    features = lax.all_to_all(inputs, TP, split_axis=2, concat_axis=0, tiled=True)
    features = features.reshape(own_tokens * tp_count, dp_count * sub_rows)
    all_heads = lax.dot_general(
        features,
        collect(value_grad, TP, 1),
        (((0,), (0,)), ((), ())),
        preferred_element_type=jnp.float32,
    )
    summed = sent_and_summed(all_heads.astype(jnp.bfloat16), DP, 0)
    local = lax.all_to_all(summed, TP, split_axis=1, concat_axis=0, tiled=True)
    total = over_axes(jnp.sum(summed * summed), DP_TP)
    limit = jnp.sqrt(jnp.float32(width * columns * lax.axis_size(TP)))
    return local * jnp.minimum(jnp.float32(1.0), limit / jnp.sqrt(total))


def solution(mesh):
    torus = Mesh(mesh.devices.reshape(4, 8, 2, 4, 2), ("dp_0", "dp_1", "dp_2", "tp_0", "tp_1"))
    return jax.shard_map(
        body,
        mesh=torus,
        in_specs=(P(DP_TP, None), P(DP_TP, None), P(DP, TP)),
        out_specs=P(DP, TP),
        check_vma=False,
    )
```

profile of v0, /device:TPU:1, one launch (start us, length us, event | category | flops | bytes accessed | tf_op | source)
XLA Modules:
  0.0 247.4 jit_solution(15634709426231722610)
XLA Ops:
  0.0 0.7 convert_element_type.16
  0.7 3.2 %copy.12 = bf16[128,8192]{0,1:T(8,128)(2,1)S(1)} copy(bf16[128,8192]{1,0:T(8,128)(2,1)} %param.3) | data formatting | bytes 4194304 | tf_op args[0]
  3.9 0.4 fusion
  4.4 1.7 copy.13
  6.1 10.5 %all-to-all-start = ((bf16[128,64,8,16]{0,3,1,2:T(8,128)(2,1)}), bf16[128,64,8,16]{0,3,1,2:T(8,128)(2,1)S(1)}, u32[]{:S(2)}, u32[]{:S(2)}) async-start(bf16[128,64,8,16]{0,3,1,2:T(8,128)(2,1)} %copy.13), calls=%async_computation | async-start | bytes 4194304 | tf_op jit(solution)/shard_map/all_to_all | solution.py:65
  16.6 0.1 copy.15
  16.7 48.7 %all-to-all-done = bf16[128,64,8,16]{0,3,1,2:T(8,128)(2,1)S(1)} async-done(((bf16[128,64,8,16]{0,3,1,2:T(8,128)(2,1)}), bf16[128,64,8,16]{0,3,1,2:T(8,128)(2,1)S(1)}, u32[]{:S(2)}, u32[]{:S(2)}) %all-to-all-start) | async-done | bytes 2097184 | tf_op jit(solution)/shard_map/all_to_all | solution.py:65
  65.4 1.6 broadcast_in_dim.4
  67.0 5.0 %all-to-all-start.1 = ((bf16[8,1024,128]{1,2,0:T(8,128)(2,1)}), bf16[8,1024,128]{1,2,0:T(8,128)(2,1)}, u32[]{:S(2)}, u32[]{:S(2)}) async-start(bf16[8,1024,128]{1,2,0:T(8,128)(2,1)} %broadcast_in_dim.4), calls=%async_computation.1 | async-start | bytes 4194304 | tf_op jit(solution)/shard_map/all_to_all | solution.py:14
  71.9 3.8 %copy.14 = bf16[8,128,64,1,16]{1,0,4,2,3:T(8,128)(2,1)} copy(bf16[8,128,64,1,16]{1,4,2,0,3:T(8,128)(2,1)S(1)} %bitcast.30) | data formatting | bytes 4194304 | tf_op jit(solution)/shard_map/all_to_all | solution.py:65
  75.7 33.4 %all-to-all-done.1 = bf16[8,1024,128]{1,2,0:T(8,128)(2,1)} async-done(((bf16[8,1024,128]{1,2,0:T(8,128)(2,1)}), bf16[8,1024,128]{1,2,0:T(8,128)(2,1)}, u32[]{:S(2)}, u32[]{:S(2)}) %all-to-all-start.1) | async-done | bytes 2097184 | tf_op jit(solution)/shard_map/all_to_all | solution.py:14
  109.1 4.6 %fusion.4 = bf16[1024,1024]{1,0:T(8,128)(2,1)S(1)} fusion(bf16[1024,1024]{0,1:T(8,128)(2,1)} %bitcast.5, bf16[128,8,8,128]{3,2,1,0:T(8,128)(2,1)} %bitcast.32), kind=kOutput, calls=%fused_computation.6 | convolution fusion | flops 2148532224 | bytes 6291456 | tf_op jit(solution)/shard_map/dot_general | solution.py:67
  113.7 75.6 %all_to_all.38 = bf16[64,16,1024]{2,1,0:T(8,128)(2,1)S(1)} all-to-all(bf16[64,16,1024]{2,1,0:T(8,128)(2,1)S(1)} %bitcast.33), channel_id=1, replica_groups=mesh['dp_0'=4,'dp_1'=8,'dp_2'=2,'tp_0'=4,'tp_1'=2] {'dp_0','dp_1','dp_2'}, dimensions={0} | all-to-all | bytes 4194304 | tf_op jit(solution)/shard_map/all_to_all | solution.py:36
  189.2 0.4 convert_reduce_fusion
  189.6 0.6 copy_bitcast_fusion
  190.2 6.9 %all-to-all-start.3 = ((f32[16,8,128]{2,0,1:T(8,128)}), f32[16,8,128]{2,0,1:T(8,128)S(1)}, u32[]{:S(2)}, u32[]{:S(2)}) async-start(f32[16,8,128]{2,0,1:T(8,128)} %copy_bitcast_fusion), calls=%async_computation.3 | async-start | bytes 131072 | tf_op jit(solution)/shard_map/all_to_all | solution.py:74
  197.1 0.7 multiply_reduce_fusion
  197.8 8.1 %psum.35 = f32[]{:T(128)} all-reduce(f32[]{:T(128)} %multiply_reduce_fusion), channel_id=1, replica_groups=mesh['dp_0'=4,'dp_1'=8,'dp_2'=2,'tp_0'=4,'tp_1'=2] {'dp_0'}, use_global_device_ids=true, to_apply=%region_2.0 | all-reduce | flops 1 | bytes 8 | tf_op jit(solution)/shard_map/psum | solution.py:42
  205.9 13.0 %psum.36 = f32[]{:T(128)} all-reduce(f32[]{:T(128)} %psum.35), channel_id=1, replica_groups=mesh['dp_0'=4,'dp_1'=8,'dp_2'=2,'tp_0'=4,'tp_1'=2] {'dp_1'}, use_global_device_ids=true, to_apply=%region_3.0 | all-reduce | flops 1 | bytes 8 | tf_op jit(solution)/shard_map/psum | solution.py:42
  218.9 4.8 %psum.37 = f32[]{:T(128)} all-reduce(f32[]{:T(128)} %psum.36), channel_id=1, replica_groups=mesh['dp_0'=4,'dp_1'=8,'dp_2'=2,'tp_0'=4,'tp_1'=2] {'dp_2'}, use_global_device_ids=true, to_apply=%region_4.0 | all-reduce | flops 1 | bytes 8 | tf_op jit(solution)/shard_map/psum | solution.py:42
  223.7 10.4 %psum.38 = f32[]{:T(128)} all-reduce(f32[]{:T(128)} %psum.37), channel_id=1, replica_groups=mesh['dp_0'=4,'dp_1'=8,'dp_2'=2,'tp_0'=4,'tp_1'=2] {'tp_0'}, use_global_device_ids=true, to_apply=%region_5.0 | all-reduce | flops 1 | bytes 8 | tf_op jit(solution)/shard_map/psum | solution.py:42
  234.0 12.0 %psum.39 = f32[]{:T(128)} all-reduce(f32[]{:T(128)} %psum.38), channel_id=1, replica_groups=mesh['dp_0'=4,'dp_1'=8,'dp_2'=2,'tp_0'=4,'tp_1'=2] {'tp_1'}, use_global_device_ids=true, to_apply=%region_6.0 | all-reduce | flops 1 | bytes 8 | tf_op jit(solution)/shard_map/psum | solution.py:42
  246.8 0.0 all-to-all-done.3
  246.8 0.6 broadcast_multiply_fusion
  (2 shorter events, 0.0 us)
Async XLA Ops:
  6.1 10.5 %copy-start = (bf16[1024,128]{1,0:T(8,128)(2,1)S(1)}, bf16[1024,128]{1,0:T(8,128)(2,1)}, u32[]{:S(2)}) copy-start(bf16[1024,128]{1,0:T(8,128)(2,1)} %param.5) | copy-start | bytes 786436
  6.1 59.3 %all-to-all-start = ((bf16[128,64,8,16]{0,3,1,2:T(8,128)(2,1)}), bf16[128,64,8,16]{0,3,1,2:T(8,128)(2,1)S(1)}, u32[]{:S(2)}, u32[]{:S(2)}) async-start(bf16[128,64,8,16]{0,3,1,2:T(8,128)(2,1)} %copy.13), calls=%async_computation | async-start | bytes 4194304 | tf_op jit(solution)/shard_map/all_to_all | solution.py:65
  67.0 42.1 %all-to-all-start.1 = ((bf16[8,1024,128]{1,2,0:T(8,128)(2,1)}), bf16[8,1024,128]{1,2,0:T(8,128)(2,1)}, u32[]{:S(2)}, u32[]{:S(2)}) async-start(bf16[8,1024,128]{1,2,0:T(8,128)(2,1)} %broadcast_in_dim.4), calls=%async_computation.1 | async-start | bytes 4194304 | tf_op jit(solution)/shard_map/all_to_all | solution.py:14
  190.2 56.5 %all-to-all-start.3 = ((f32[16,8,128]{2,0,1:T(8,128)}), f32[16,8,128]{2,0,1:T(8,128)S(1)}, u32[]{:S(2)}, u32[]{:S(2)}) async-start(f32[16,8,128]{2,0,1:T(8,128)} %copy_bitcast_fusion), calls=%async_computation.3 | async-start | bytes 131072 | tf_op jit(solution)/shard_map/all_to_all | solution.py:74
where the time goes:
time: 248 us; the launch traced here: 247 us
  blocking collectives  124 us (50%)
  waiting for transfers between devices  82.1 us (33%)
  starting transfers between devices  22.3 us (9%)
  local copies, waits for them, and re-layouts  11.1 us (4%)
  matrix products  4.58 us (2%)
  other arithmetic  2.82 us (1%)
    all_to_all x1, blocking collectives, sent_and_summed(): lax.all_to_all(pieces, axis, split_axis=0, concat_axis=0, tiled=True)  75.6 us
    all_to_all x1, waiting for transfers between devices, body(): lax.all_to_all(inputs, TP, split_axis=2, concat_axis=0, tiled=True)  48.7 us
    psum x5, blocking collectives, over_axes(): shard = lax.psum(shard, axis)  48.2 us
    all_to_all x1, waiting for transfers between devices, copy_for_each(): return lax.all_to_all(copies, axis, split_axis=0, concat_axis=0, tiled=True)  33.4 us
    all_to_all x1, starting transfers between devices, body(): lax.all_to_all(inputs, TP, split_axis=2, concat_axis=0, tiled=True)  10.5 us
    all_to_all x1, starting transfers between devices, body(): local = lax.all_to_all(summed, TP, split_axis=1, concat_axis=0, tiled=True)  6.87 us
    all_to_all x1, starting transfers between devices, copy_for_each(): return lax.all_to_all(copies, axis, split_axis=0, concat_axis=0, tiled=True)  4.97 us
  transfers between devices with their start and end apart: 3, of which 2 were waited for; matrix products, arithmetic and copies ran while one was open for 2% of the time, Pallas kernels for 0%

commit v1 on v0

--- a/solution.py
+++ b/solution.py
@@ -39,7 +39,7 @@
 
 def over_axes(shard, axes):
     for axis in axes:
-        shard = lax.psum(shard, axis)
+        shard = jnp.sum(lax.all_gather(shard, axis), axis=0)
     return shard
 
 

time: 248 us -> 261 us (1.052)
  blocking collectives: 124 us -> 44.7 us
  waiting for transfers between devices: 82.1 us -> 129 us
  starting transfers between devices: 22.3 us -> 50.2 us
  local copies, waits for them, and re-layouts: 11.1 us -> 24.2 us
  other arithmetic: 2.82 us -> 5.43 us
    all_to_all x1 -> x0, blocking collectives: 75.6 us -> none  [sent_and_summed(): lax.all_to_all(pieces, axis, split_axis=0, concat_axis=0, tiled=True)]
    psum x5 -> x0, blocking collectives: 48.2 us -> none  [over_axes(): shard = lax.psum(shard, axis)]
    all_to_all x0 -> x1, waiting for transfers between devices: none -> 46.5 us  [sent_and_summed(): lax.all_to_all(pieces, axis, split_axis=0, concat_axis=0, tiled=True)]
    unnamed x0 -> x5, blocking collectives: none -> 44.7 us
    all_to_all x0 -> x1, starting transfers between devices: none -> 27.9 us  [sent_and_summed(): lax.all_to_all(pieces, axis, split_axis=0, concat_axis=0, tiled=True)]
    unnamed x4 -> x21, local copies, waits for them, and re-layouts: 3.36 us -> 16.5 us
    reduce_sum x0 -> x5, other arithmetic: none -> 3.42 us  [over_axes(): shard = jnp.sum(lax.all_gather(shard, axis), axis=0)]
  transfers between devices with their start and end apart: 3 -> 4, of which waited for: 2 -> 3; matrix products, arithmetic and copies ran while one was open for 2% -> 8% of each run, Pallas kernels for 0% -> 0%
where the time goes in v1:
time: 261 us; the launch traced here: 260 us
  waiting for transfers between devices  129 us (49%)
  starting transfers between devices  50.2 us (19%)
  blocking collectives  44.7 us (17%)
  local copies, waits for them, and re-layouts  24.2 us (9%)
  matrix products  5.92 us (2%)
  other arithmetic  5.43 us (2%)
    all_to_all x1, waiting for transfers between devices, body(): lax.all_to_all(inputs, TP, split_axis=2, concat_axis=0, tiled=True)  48.7 us
    all_to_all x1, waiting for transfers between devices, sent_and_summed(): lax.all_to_all(pieces, axis, split_axis=0, concat_axis=0, tiled=True)  46.5 us
    unnamed x5, blocking collectives  44.7 us
    all_to_all x1, waiting for transfers between devices, copy_for_each(): return lax.all_to_all(copies, axis, split_axis=0, concat_axis=0, tiled=True)  33.4 us
    all_to_all x1, starting transfers between devices, sent_and_summed(): lax.all_to_all(pieces, axis, split_axis=0, concat_axis=0, tiled=True)  27.9 us
    unnamed x21, local copies, waits for them, and re-layouts  16.5 us
    all_to_all x1, starting transfers between devices, body(): lax.all_to_all(inputs, TP, split_axis=2, concat_axis=0, tiled=True)  10.5 us
    all_to_all x1, starting transfers between devices, body(): local = lax.all_to_all(summed, TP, split_axis=1, concat_axis=0, tiled=True)  6.87 us
  transfers between devices with their start and end apart: 4, of which 3 were waited for; matrix products, arithmetic and copies ran while one was open for 8% of the time, Pallas kernels for 0%

profile of v1, /device:TPU:1, one launch (start us, length us, event | category | flops | bytes accessed | tf_op | source)
XLA Modules:
  0.0 259.9 jit_solution(656903706584573158)
XLA Ops:
  0.0 3.2 %copy.12 = bf16[128,8192]{0,1:T(8,128)(2,1)S(1)} copy(bf16[128,8192]{1,0:T(8,128)(2,1)} %param.3) | data formatting | bytes 4194304 | tf_op args[0]
  3.7 1.7 copy.13
  5.4 10.5 %all-to-all-start = ((bf16[128,64,8,16]{0,3,1,2:T(8,128)(2,1)}), bf16[128,64,8,16]{0,3,1,2:T(8,128)(2,1)S(1)}, u32[]{:S(2)}, u32[]{:S(2)}) async-start(bf16[128,64,8,16]{0,3,1,2:T(8,128)(2,1)} %copy.13), calls=%async_computation | async-start | bytes 4194304 | tf_op jit(solution)/shard_map/all_to_all | solution.py:65
  16.0 48.7 %all-to-all-done = bf16[128,64,8,16]{0,3,1,2:T(8,128)(2,1)S(1)} async-done(((bf16[128,64,8,16]{0,3,1,2:T(8,128)(2,1)}), bf16[128,64,8,16]{0,3,1,2:T(8,128)(2,1)S(1)}, u32[]{:S(2)}, u32[]{:S(2)}) %all-to-all-start) | async-done | bytes 2097184 | tf_op jit(solution)/shard_map/all_to_all | solution.py:65
  64.7 1.6 broadcast_in_dim.4
  66.3 5.0 %all-to-all-start.1 = ((bf16[8,1024,128]{1,2,0:T(8,128)(2,1)}), bf16[8,1024,128]{1,2,0:T(8,128)(2,1)}, u32[]{:S(2)}, u32[]{:S(2)}) async-start(bf16[8,1024,128]{1,2,0:T(8,128)(2,1)} %broadcast_in_dim.4), calls=%async_computation.1 | async-start | bytes 4194304 | tf_op jit(solution)/shard_map/all_to_all | solution.py:14
  71.3 3.7 %copy.14 = bf16[8,128,64,1,16]{1,0,4,2,3:T(8,128)(2,1)} copy(bf16[8,128,64,1,16]{1,4,2,0,3:T(8,128)(2,1)S(1)} %bitcast.40) | data formatting | bytes 4194304 | tf_op jit(solution)/shard_map/all_to_all | solution.py:65
  75.0 33.4 %all-to-all-done.1 = bf16[8,1024,128]{1,2,0:T(8,128)(2,1)} async-done(((bf16[8,1024,128]{1,2,0:T(8,128)(2,1)}), bf16[8,1024,128]{1,2,0:T(8,128)(2,1)}, u32[]{:S(2)}, u32[]{:S(2)}) %all-to-all-start.1) | async-done | bytes 2097184 | tf_op jit(solution)/shard_map/all_to_all | solution.py:14
  108.4 5.9 %fusion.4 = bf16[1024,1024]{1,0:T(8,128)(2,1)} fusion(bf16[1024,1024]{0,1:T(8,128)(2,1)} %bitcast.5, bf16[128,8,8,128]{3,2,1,0:T(8,128)(2,1)} %bitcast.43), kind=kOutput, calls=%fused_computation.6 | convolution fusion | flops 2148532224 | bytes 6291456 | tf_op jit(solution)/shard_map/dot_general | solution.py:67
  114.4 27.9 %all-to-all-start.2 = ((bf16[64,16,1024]{2,1,0:T(8,128)(2,1)}), bf16[64,16,1024]{2,1,0:T(8,128)(2,1)S(1)}, u32[]{:S(2)}, u32[]{:S(2)}) async-start(bf16[64,16,1024]{2,1,0:T(8,128)(2,1)} %bitcast.42), calls=%async_computation.2 | async-start | bytes 4194304 | tf_op jit(solution)/shard_map/all_to_all | solution.py:36
  142.3 1.3 dynamic-slice
  143.6 46.5 %all-to-all-done.2 = bf16[64,16,1024]{2,1,0:T(8,128)(2,1)S(1)} async-done(((bf16[64,16,1024]{2,1,0:T(8,128)(2,1)}), bf16[64,16,1024]{2,1,0:T(8,128)(2,1)S(1)}, u32[]{:S(2)}, u32[]{:S(2)}) %all-to-all-start.2) | async-done | bytes 2097184 | tf_op jit(solution)/shard_map/all_to_all | solution.py:36
  191.1 6.9 %all-to-all-start.3 = ((f32[16,8,128]{2,0,1:T(8,128)}), f32[16,8,128]{2,0,1:T(8,128)S(1)}, u32[]{:S(2)}, u32[]{:S(2)}) async-start(f32[16,8,128]{2,0,1:T(8,128)} %copy_bitcast_fusion), calls=%async_computation.3 | async-start | bytes 131072 | tf_op jit(solution)/shard_map/all_to_all | solution.py:74
  198.6 1.4 dynamic-update-slice
  200.0 1.3 dynamic-slice.1
  201.2 7.1 %all-reduce = f32[4]{0:T(128)S(1)} all-reduce(f32[4]{0:T(128)S(1)} %dynamic-update-slice), channel_id=1, replica_groups=mesh['dp_0'=4,'dp_1'=8,'dp_2'=2,'tp_0'=4,'tp_1'=2] {'dp_0'}, use_global_device_ids=true, to_apply=%add | all-reduce | flops 4 | bytes 32
  209.0 1.4 dynamic-update-slice.1
  211.6 12.0 %all-reduce.1 = f32[8]{0:T(128)S(1)} all-reduce(f32[8]{0:T(128)S(1)} %dynamic-update-slice.1), channel_id=1, replica_groups=mesh['dp_0'=4,'dp_1'=8,'dp_2'=2,'tp_0'=4,'tp_1'=2] {'dp_1'}, use_global_device_ids=true, to_apply=%add.1 | all-reduce | flops 8 | bytes 64
  224.3 1.4 dynamic-update-slice.2
  226.9 3.8 %all-reduce.2 = f32[2]{0:T(128)S(1)} all-reduce(f32[2]{0:T(128)S(1)} %dynamic-update-slice.2), channel_id=1, replica_groups=mesh['dp_0'=4,'dp_1'=8,'dp_2'=2,'tp_0'=4,'tp_1'=2] {'dp_2'}, use_global_device_ids=true, to_apply=%add.2 | all-reduce | flops 2 | bytes 16
  231.5 1.4 dynamic-update-slice.3
  234.1 10.4 %all-reduce.3 = f32[4]{0:T(128)S(1)} all-reduce(f32[4]{0:T(128)S(1)} %dynamic-update-slice.3), channel_id=1, replica_groups=mesh['dp_0'=4,'dp_1'=8,'dp_2'=2,'tp_0'=4,'tp_1'=2] {'tp_0'}, use_global_device_ids=true, to_apply=%add.3 | all-reduce | flops 4 | bytes 32
  245.2 1.4 dynamic-update-slice.4
  246.5 11.3 %all-reduce.4 = f32[2]{0:T(128)S(1)} all-reduce(f32[2]{0:T(128)S(1)} %dynamic-update-slice.4), channel_id=1, replica_groups=mesh['dp_0'=4,'dp_1'=8,'dp_2'=2,'tp_0'=4,'tp_1'=2] {'tp_1'}, use_global_device_ids=true, to_apply=%add.4 | all-reduce | flops 2 | bytes 16
  (25 shorter events, 10.0 us)
Async XLA Ops:
  0.0 3.2 %copy-start.1 = (bf16[128,64]{0,1:T(8,128)(2,1)S(1)}, bf16[128,64]{0,1:T(8,128)(2,1)}, u32[]{:S(2)}) copy-start(bf16[128,64]{0,1:T(8,128)(2,1)} %param.4) | copy-start | bytes 49156
  5.4 10.5 %copy-start = (bf16[1024,128]{1,0:T(8,128)(2,1)S(1)}, bf16[1024,128]{1,0:T(8,128)(2,1)}, u32[]{:S(2)}) copy-start(bf16[1024,128]{1,0:T(8,128)(2,1)} %param.5) | copy-start | bytes 786436
  5.4 59.3 %all-to-all-start = ((bf16[128,64,8,16]{0,3,1,2:T(8,128)(2,1)}), bf16[128,64,8,16]{0,3,1,2:T(8,128)(2,1)S(1)}, u32[]{:S(2)}, u32[]{:S(2)}) async-start(bf16[128,64,8,16]{0,3,1,2:T(8,128)(2,1)} %copy.13), calls=%async_computation | async-start | bytes 4194304 | tf_op jit(solution)/shard_map/all_to_all | solution.py:65
  66.3 42.1 %all-to-all-start.1 = ((bf16[8,1024,128]{1,2,0:T(8,128)(2,1)}), bf16[8,1024,128]{1,2,0:T(8,128)(2,1)}, u32[]{:S(2)}, u32[]{:S(2)}) async-start(bf16[8,1024,128]{1,2,0:T(8,128)(2,1)} %broadcast_in_dim.4), calls=%async_computation.1 | async-start | bytes 4194304 | tf_op jit(solution)/shard_map/all_to_all | solution.py:14
  114.4 75.8 %all-to-all-start.2 = ((bf16[64,16,1024]{2,1,0:T(8,128)(2,1)}), bf16[64,16,1024]{2,1,0:T(8,128)(2,1)S(1)}, u32[]{:S(2)}, u32[]{:S(2)}) async-start(bf16[64,16,1024]{2,1,0:T(8,128)(2,1)} %bitcast.42), calls=%async_computation.2 | async-start | bytes 4194304 | tf_op jit(solution)/shard_map/all_to_all | solution.py:36
  191.1 68.1 %all-to-all-start.3 = ((f32[16,8,128]{2,0,1:T(8,128)}), f32[16,8,128]{2,0,1:T(8,128)S(1)}, u32[]{:S(2)}, u32[]{:S(2)}) async-start(f32[16,8,128]{2,0,1:T(8,128)} %copy_bitcast_fusion), calls=%async_computation.3 | async-start | bytes 131072 | tf_op jit(solution)/shard_map/all_to_all | solution.py:74
